TPU v7x, 32 devices: a whole 2x2x4 slice. The times are simulated.
32 devices in a mesh: dp: 4 (over x, core), query: 8 (over z, y).
Axes of the slice: x: 2, y: 2, z: 4, core: 2. Of those that a mesh axis runs over, the one named last changes fastest.
Arguments:
- corpus: bfloat16 [131072, 1024], P(('dp', 'query')), may hold values from -6 to 6
- queries: float32 [512, 1024], P('query'), may hold values from -800 to 800
- cand_ids: int32 [32, 512, 8], P(('dp', 'query')), may hold values from 0 to 4095
- cand_counts: int32 [32, 512], P(('dp', 'query')), may hold values from 1 to 8
Outputs:
- log_total: float32 [512], P('query')
- pooled: float32 [512, 1024], P('query')
All inputs are finite; a program needn't handle non-finite values.
Results may differ from a plain program's by a relative error of at most 0.0003.
Values may be sent and summed in bfloat16 or wider, within the bound.
A program may use at most 128 MiB of HBM per device.

v0:
```python
import jax
import jax.numpy as jnp
from jax import lax
from jax.sharding import PartitionSpec as P


def combined_all(value, axis, join):
    pieces = jax.tree.map(lambda part: lax.all_gather(part, axis), value)
    head = jax.tree.map(lambda part: part[0], pieces)
    tail = jax.tree.map(lambda part: part[1:], pieces)
    total, _ = lax.scan(lambda total, section: (join(total, section), None), head, tail)
    return total


def combine_parts(first, second):
    best_a, total_a, weighted_a = first
    best_b, total_b, weighted_b = second
    best = jnp.maximum(best_a, best_b)
    scale_a = jnp.exp(best_a - best)
    scale_b = jnp.exp(best_b - best)
    return (
        best,
        total_a * scale_a + total_b * scale_b,
        weighted_a * scale_a[..., None] + weighted_b * scale_b[..., None],
    )


def body(corpus, queries, cand_ids, cand_counts):
    n_owner = lax.axis_size("query")
    q_local = queries.shape[0]
    width = queries.shape[1]
    slots = cand_ids.shape[2]
    inverse_root = jnp.float32(1.0) / jnp.sqrt(jnp.float32(width))
    slot_index = jnp.arange(slots, dtype=jnp.int32)
    picked = corpus[cand_ids[0]]
    every_query = lax.all_gather(queries, "query", axis=0, tiled=True)
    widened = picked.astype(jnp.float32)
    scores = (
        jnp.einsum("qcd,qd->qc", widened, every_query, precision=lax.Precision.HIGHEST)
        * inverse_root
    )
    alive_mask = slot_index[None, :] < cand_counts[0][:, None]
    masked = jnp.where(alive_mask, scores, jnp.float32(-1e30))
    part_best = jnp.max(masked, axis=1)
    weights = jnp.where(alive_mask, jnp.exp(masked - part_best[:, None]), jnp.float32(0.0))
    part_total = jnp.sum(weights, axis=1)
    part_weighted = jnp.einsum("qc,qcd->qd", weights, widened, precision=lax.Precision.HIGHEST)
    got_best, got_total, got_weighted = (
        lax.all_to_all(
            part_best.reshape(n_owner, q_local), "query", split_axis=0, concat_axis=0, tiled=True
        ),
        lax.all_to_all(
            part_total.reshape(n_owner, q_local), "query", split_axis=0, concat_axis=0, tiled=True
        ),
        lax.all_to_all(
            part_weighted.reshape(n_owner, q_local, width),
            "query",
            split_axis=0,
            concat_axis=0,
            tiled=True,
        ),
    )
    best = jnp.max(got_best, axis=0)
    rescale = jnp.exp(got_best - best[None, :])
    total = jnp.sum(got_total * rescale, axis=0)
    weighted = jnp.sum(got_weighted * rescale[:, :, None], axis=0)
    best, total, weighted = combined_all((best, total, weighted), "dp", combine_parts)
    return (best + jnp.log(total), weighted / total[:, None])


def solution(mesh):
    in_specs = (
        P(("dp", "query"), None),
        P("query", None),
        P(("dp", "query"), None, None),
        P(("dp", "query"), None),
    )
    out_specs = (P("query"), P("query", None))
    return jax.shard_map(body, mesh=mesh, in_specs=in_specs, out_specs=out_specs, check_vma=False)
```

profile of v0, /device:TPU:1, one launch (start us, length us, event | category | flops | bytes accessed | tf_op | source)
XLA Modules:
  0.0 185.1 jit_solution(17398410263918070264)
XLA Ops:
  7.2 0.0 all-gather.6.cloned.1.call-start
  7.2 0.7 all-gather.6.cloned.1.call-update
  7.9 0.7 compare_select_fusion
  8.6 0.1 copy.9
  8.8 0.2 reshape.67
  8.9 25.3 %gather_fusion = bf16[4096,1024]{1,0:T(8,128)(2,1)} fusion(bf16[4096,1024]{1,0:T(8,128)(2,1)} %param.6, s32[4096]{0:T(1024)S(1)} %broadcast_clamp_fusion), kind=kCustom, calls=%fused_computation | custom fusion | bytes 16793600 | tf_op jit(solution)/shard_map/gather | solution.py:35
  34.3 0.0 copy-start
  34.3 25.1 %all-gather.6.cloned.1.call-done = f32[512,1024]{1,0:T(8,128)} async-done(((f32[64,1024]{1,0:T(8,128)}), f32[512,1024]{1,0:T(8,128)}) %all-gather.6.cloned.1.call-update) | async-done | bytes 2097168 | tf_op jit(solution)/shard_map/all_gather | solution.py:36
  59.4 19.1 %fusion.6 = f32[512,1,8]{2,1,0:T(1,128)S(1)} fusion(bf16[4096,1024]{1,0:T(8,128)(2,1)} %gather_fusion, f32[512,1024,1]{1,0,2:T(8,128)} %bitcast.60), kind=kOutput, calls=%fused_computation.12 | convolution fusion | flops 50331648 | bytes 10502144 | tf_op jit(solution)/shard_map/qcd,qd->qc/dot_general | solution.py:39
  78.5 0.1 copy.11
  78.6 0.0 copy-done
  78.7 0.7 all_to_all.21
  79.3 4.2 %all-to-all-start.1 = ((f32[8,1,64]{2,1,0:T(1,128)}), f32[8,1,64]{2,1,0:T(1,128)S(1)}, u32[]{:S(2)}, u32[]{:S(2)}) async-start(f32[8,1,64]{2,1,0:T(1,128)} %all_to_all.21), calls=%async_computation.1 | async-start | bytes 8192 | tf_op jit(solution)/shard_map/all_to_all | solution.py:52
  83.6 0.7 all_to_all.19
  84.2 0.1 copy.12
  84.4 4.5 %all-to-all-done.1 = f32[8,1,64]{2,1,0:T(1,128)S(1)} async-done(((f32[8,1,64]{2,1,0:T(1,128)}), f32[8,1,64]{2,1,0:T(1,128)S(1)}, u32[]{:S(2)}, u32[]{:S(2)}) %all-to-all-start.1) | async-done | bytes 2080 | tf_op jit(solution)/shard_map/all_to_all | solution.py:52
  88.9 3.3 %all-to-all-start = ((f32[8,1,64]{2,1,0:T(1,128)}), f32[8,1,64]{2,1,0:T(1,128)S(1)}, u32[]{:S(2)}, u32[]{:S(2)}) async-start(f32[8,1,64]{2,1,0:T(1,128)} %all_to_all.19), calls=%async_computation | async-start | bytes 8192 | tf_op jit(solution)/shard_map/all_to_all | solution.py:49
  92.2 9.3 %fusion.8 = f32[512,1,1024]{2,1,0:T(1,128)S(1)} fusion(f32[512,8,1]{1,2,0:T(1,128)S(1)} %copy.12, bf16[4096,1024]{1,0:T(8,128)(2,1)} %gather_fusion), kind=kOutput, calls=%fused_computation.14 | convolution fusion | flops 50331648 | bytes 10502144 | tf_op jit(solution)/shard_map/qc,qcd->qd/dot_general | solution.py:47
  101.5 0.0 copy-start.1
  101.5 1.8 copy.13
  103.3 0.0 all-to-all-done
  103.3 5.4 %all-to-all-start.2 = ((f32[8,64,1024]{2,1,0:T(8,128)}), f32[8,64,1024]{2,1,0:T(8,128)S(1)}, u32[]{:S(2)}, u32[]{:S(2)}) async-start(f32[8,64,1024]{2,1,0:T(8,128)} %bitcast.13), calls=%async_computation.2 | async-start | bytes 4194304 | tf_op jit(solution)/shard_map/all_to_all | solution.py:55
  108.7 0.0 all-gather.8.cloned.1.call-start
  108.8 45.1 %all-to-all-done.2 = f32[8,64,1024]{2,1,0:T(8,128)S(1)} async-done(((f32[8,64,1024]{2,1,0:T(8,128)}), f32[8,64,1024]{2,1,0:T(8,128)S(1)}, u32[]{:S(2)}, u32[]{:S(2)}) %all-to-all-start.2) | async-done | bytes 2097184 | tf_op jit(solution)/shard_map/all_to_all | solution.py:55
  153.9 0.9 multiply_reduce_fusion
  154.8 0.0 all-gather.8.cloned.1.call-update
  154.8 0.0 copy-done.1
  154.8 0.6 dynamic-slice
  156.1 0.2 dynamic-update-slice
  156.3 0.2 dynamic-update-slice.1
  156.6 9.2 %all-reduce.2 = (f32[256]{0:T(256)S(1)}, f32[256]{0:T(256)S(1)}) all-reduce(f32[256]{0:T(256)S(1)} %dynamic-update-slice, f32[256]{0:T(256)S(1)} %dynamic-update-slice.1), channel_id=2, replica_groups=mesh['dp'=4,'query'=8] {'dp'}, use_global_device_ids=true, to_apply=%add | all-reduce | flops 512 | bytes 4096
  165.7 0.1 slice.27
  165.8 0.1 slice.28
  165.9 0.1 reshape.83
  166.0 0.1 reshape.84
  166.0 8.3 %all-gather.8.cloned.1.call-done = f32[256,1024]{1,0:T(8,128)} async-done(((f32[64,1024]{1,0:T(8,128)}), f32[256,1024]{1,0:T(8,128)}) %all-gather.8.cloned.1.call-update) | async-done | bytes 1048592 | tf_op jit(solution)/shard_map/all_gather | solution.py:8
  174.3 1.2 slice.33
  175.5 1.0 slice.32
  176.5 0.5 while.14
  176.5 0.1 fusion.20
  176.7 0.1 fusion.20
  176.9 0.1 fusion.20
  177.0 0.8 broadcast_divide_fusion
  177.8 0.5 log_add_fusion
  (12 shorter events, 0.2 us)
Async XLA Ops:
  7.2 52.2 %all-gather.6.cloned.1.call-start = ((), (), s32[]{:S(2)}) async-start(), calls=%async_computation.3 | async-start | bytes 2359296 | tf_op jit(solution)/shard_map/all_gather | solution.py:36
  34.3 44.3 %copy-start = (s32[1,512]{1,0:T(1,128)S(1)}, s32[1,512]{1,0:T(1,128)}, u32[]{:S(2)}) copy-start(s32[1,512]{1,0:T(1,128)} %param.9) | copy-start | bytes 6148
  79.3 9.5 %all-to-all-start.1 = ((f32[8,1,64]{2,1,0:T(1,128)}), f32[8,1,64]{2,1,0:T(1,128)S(1)}, u32[]{:S(2)}, u32[]{:S(2)}) async-start(f32[8,1,64]{2,1,0:T(1,128)} %all_to_all.21), calls=%async_computation.1 | async-start | bytes 8192 | tf_op jit(solution)/shard_map/all_to_all | solution.py:52
  88.9 14.4 %all-to-all-start = ((f32[8,1,64]{2,1,0:T(1,128)}), f32[8,1,64]{2,1,0:T(1,128)S(1)}, u32[]{:S(2)}, u32[]{:S(2)}) async-start(f32[8,1,64]{2,1,0:T(1,128)} %all_to_all.19), calls=%async_computation | async-start | bytes 8192 | tf_op jit(solution)/shard_map/all_to_all | solution.py:49
  101.5 53.4 %copy-start.1 = (u32[32]{0:T(128)S(1)}, u32[32]{0:T(128)}, u32[]{:S(2)}) copy-start(u32[32]{0:T(128)} %constant.27) | copy-start | bytes 388
  103.3 50.6 %all-to-all-start.2 = ((f32[8,64,1024]{2,1,0:T(8,128)}), f32[8,64,1024]{2,1,0:T(8,128)S(1)}, u32[]{:S(2)}, u32[]{:S(2)}) async-start(f32[8,64,1024]{2,1,0:T(8,128)} %bitcast.13), calls=%async_computation.2 | async-start | bytes 4194304 | tf_op jit(solution)/shard_map/all_to_all | solution.py:55
  108.7 65.7 %all-gather.8.cloned.1.call-start = ((), (), s32[]{:S(2)}) async-start(), calls=%async_computation.4 | async-start | bytes 1310720 | tf_op jit(solution)/shard_map/all_gather | solution.py:8
Sparse Core Ops, SparseCore 0:
  10.1 49.2 all-gather.5
  154.9 19.3 all-gather.7
where the time goes:
time: 186 us; the launch traced here: 185 us
  waiting for transfers between devices  83.8 us (45%)
  local copies, waits for them, and re-layouts  32.5 us (17%)
  matrix products  28.4 us (15%)
  between operations  14.8 us (8%)
  starting transfers between devices  13 us (7%)
  blocking collectives  9.18 us (5%)
  other arithmetic  3.48 us (2%)
    all_to_all x1, waiting for transfers between devices, body(): lax.all_to_all(part_weighted.reshape(n_owner, q_local, width), 'query', s...  45.1 us
    gather x1, local copies, waits for them, and re-layouts, body(): picked = corpus[cand_ids[0]]  25.3 us
    all_gather x1, waiting for transfers between devices, body(): every_query = lax.all_gather(queries, 'query', axis=0, tiled=True)  25.1 us
    dot_general x1, matrix products, body(): jnp.einsum('qcd,qd->qc', widened, every_query, precision=lax.Precision.HI...  19.1 us
    dot_general x1, matrix products, body(): jnp.einsum('qc,qcd->qd', weights, widened, precision=lax.Precision.HIGHEST)  9.26 us
    unnamed x1, blocking collectives  9.18 us
    all_gather x1, waiting for transfers between devices, combined_all(): pieces = jax.tree.map(lambda part: lax.all_gather(part, axis), value)  8.29 us
    all_to_all x1, starting transfers between devices, body(): lax.all_to_all(part_weighted.reshape(n_owner, q_local, width), 'query', s...  5.37 us
  transfers between devices with their start and end apart: 5, of which 4 were waited for; matrix products, arithmetic and copies ran while one was open for 21% of the time, Pallas kernels for 0%

commit v1 on v0

v1 whole, which is shorter than its diff:
```python
import functools

import jax
import jax.numpy as jnp
from jax import lax
from jax.experimental import pallas as pl
from jax.experimental.pallas import tpu as pltpu
from jax.sharding import PartitionSpec as P

MESH = pl.DeviceIdType.MESH
LANES = 128
SUB = 8
NEG = -1e30
CHUNK = 256
SLOTS = 4


def low_bit(k):
    return (k & -k).bit_length() - 1


def halves_combine(a, b, step, mask):
    u = jnp.where(mask, a, b)
    v = jnp.where(mask, b, a)
    return u + pltpu.roll(v, step, 0)


def sub_reduce(x, op):
    for step in (4, 2, 1):
        x = op(x, pltpu.roll(x, step, 0))
    return x


def kernel(
    cfg, ids, counts, q_hbm, corpus_hbm, out_ref, log_ref,
    c32, stage, allq, acc, rcore, rbits, rx, fin,
    stage_sem, own_sem, ag_send, ag_recv, agc_send, agc_recv,
    rc_send, rc_recv, rb_send, rb_recv, rx_send, rx_recv, fin_send, fin_recv,
):
    n, d, half_rows, slots, tiles, rows, inv_root = cfg
    nbits = n.bit_length() - 1
    dbits = d.bit_length() - 1
    me = lax.axis_index("query")
    dp = lax.axis_index("dp")
    core = lax.rem(dp, 2)
    other = 1 - core
    stat = tiles * SUB
    group_rows = (tiles + 1) * SUB
    groups = half_rows // SUB
    piece = groups * group_rows
    qpiece = half_rows * tiles

    def flip(x, bit):
        return x + (1 << bit) - 2 * (1 << bit) * lax.rem(x // (1 << bit), 2)

    def owner(k):
        s = me
        for b in range(nbits):
            if k >> b & 1:
                s = flip(s, b)
        return s

    def q_to(bit):
        return {"query": flip(me, bit)}

    def d_to(bit):
        return {"dp": flip(dp, bit)}

    barrier = pltpu.get_barrier_semaphore()
    for b in range(nbits):
        pl.semaphore_signal(barrier, inc=1, device_id=q_to(b), device_id_type=MESH)
    for b in range(dbits):
        pl.semaphore_signal(barrier, inc=1, device_id=d_to(b), device_id_type=MESH)

    def stage_copy(i, slot):
        return pltpu.make_async_copy(
            corpus_hbm.at[pl.ds(i * CHUNK, CHUNK), :], stage.at[slot], stage_sem.at[slot]
        )

    for i in range(SLOTS):
        stage_copy(i, i).start()

    def q_at(s, half):
        return pl.multiple_of((s * 2 + half) * qpiece, SUB)

    own_copy = pltpu.make_async_copy(
        q_hbm, allq.at[pl.ds(pl.multiple_of(me * (2 * qpiece), SUB), 2 * qpiece), :], own_sem
    )
    own_copy.start()
    pl.semaphore_wait(barrier, nbits + dbits)

    started = []

    def remote(src, dst, send, recv, to):
        copy = pltpu.make_async_remote_copy(
            src_ref=src, dst_ref=dst, send_sem=send, recv_sem=recv,
            device_id=to, device_id_type=MESH,
        )
        copy.start()
        started.append(copy)
        return copy

    def ag_piece(k, half):
        return allq.at[pl.ds(q_at(owner(k), half), qpiece), :]

    def ag_forward(k):
        for b in reversed(range(low_bit(k) if k else nbits)):
            if k:
                src = ag_piece(k, core)
            else:
                src = q_hbm.at[pl.ds(pl.multiple_of(core * qpiece, SUB), qpiece), :]
            j = k | 1 << b
            remote(src, ag_piece(k, core), ag_send.at[j], ag_recv.at[j], q_to(b))
        if k:
            remote(ag_piece(k, core), ag_piece(k, core), agc_send.at[k], agc_recv.at[k], d_to(0))

    def arrived(k, half, send, recv, to):
        pltpu.make_async_remote_copy(
            src_ref=ag_piece(k, half), dst_ref=ag_piece(k, half), send_sem=send.at[k],
            recv_sem=recv.at[k], device_id=to, device_id_type=MESH,
        ).wait_recv()

    def relay(k):
        arrived(k, core, ag_send, ag_recv, q_to(low_bit(k)))
        ag_forward(k)

    ag_forward(0)

    n_chunks = rows // CHUNK
    flat = c32.reshape(rows * tiles, LANES)

    def convert(i, _):
        slot = lax.rem(i, SLOTS)
        stage_copy(i, slot).wait()

        def block(r, _):
            r0 = pl.multiple_of(r * 16, 16)
            to = pl.multiple_of((i * CHUNK + r * 16) * tiles, SUB)
            for j in range(tiles):
                x = stage[slot, pl.ds(r0, 16), j * LANES : (j + 1) * LANES].astype(jnp.float32)
                flat[pl.ds(to + j, SUB, stride=tiles), :] = x[:SUB]
                flat[pl.ds(to + SUB * tiles + j, SUB, stride=tiles), :] = x[SUB:]
            return 0

        lax.fori_loop(0, CHUNK // 16, block, 0)

        @pl.when(i + SLOTS < n_chunks)
        def _():
            stage_copy(i + SLOTS, slot).start()

        return 0

    relays = sorted(range(1, n), key=lambda k: (k.bit_count(), -low_bit(k), k))
    pending = list(relays)
    parts = 4
    for part in range(parts):
        lax.fori_loop(part * n_chunks // parts, (part + 1) * n_chunks // parts, convert, 0)
        if part and pending:
            relay(pending.pop(0))

    sub = lax.broadcasted_iota(jnp.int32, (SUB, LANES), 0)
    lane = lax.broadcasted_iota(jnp.int32, (SUB, LANES), 1)
    masks = {4: sub < 4, 2: lax.rem(sub, 4) < 2, 1: lax.rem(sub, 2) < 1}

    def acc_at(s, half):
        return pl.multiple_of((s * 2 + half) * piece, SUB)

    def compute(k, half):
        s = owner(k)
        q0 = q_at(s, half)
        a0 = acc_at(s, half)
        first = s * (2 * half_rows) + half * half_rows

        def row(index):
            return c32[ids[index]]

        def group(g, _):
            query = first + g * SUB
            weights, stats = [], jnp.zeros((SUB, LANES), jnp.float32)
            for qi in range(SUB):
                at = (query + qi) * slots
                q = allq[pl.ds(pl.multiple_of(q0 + (g * SUB + qi) * tiles, SUB), tiles), :]
                level = [row(at + c) * q for c in range(slots)]
                for step in (1, 2, 4):
                    level = [
                        halves_combine(a, b, step, masks[step])
                        for a, b in zip(level[::2], level[1::2])
                    ]
                score = jnp.sum(level[0], axis=1, keepdims=True) * inv_root
                score = jnp.broadcast_to(score, (SUB, LANES))
                live = sub < counts[query + qi]
                score = jnp.where(live, score, NEG)
                best = sub_reduce(score, jnp.maximum)
                weight = jnp.where(live, jnp.exp(score - best), 0.0)
                total = sub_reduce(weight, jnp.add)
                weights.append(weight)
                stats = jnp.where(sub == qi, jnp.where(lane < LANES // 2, best, total), stats)
            base = pl.multiple_of(a0 + g * group_rows, SUB)
            for qi in range(SUB):
                at = (query + qi) * slots
                terms = [
                    jnp.broadcast_to(weights[qi][c : c + 1, :], (SUB, LANES)) * row(at + c)
                    for c in range(slots)
                ]
                while len(terms) > 1:
                    terms = [a + b for a, b in zip(terms[::2], terms[1::2])]
                acc[pl.ds(base + qi, tiles, stride=SUB), :] = terms[0]
            acc[pl.ds(pl.multiple_of(base + stat, SUB), SUB), :] = stats
            return 0

        lax.fori_loop(0, groups, group, 0)

    def split(x):
        turned = pltpu.roll(x, LANES // 2, 1)
        left = lane < LANES // 2
        return jnp.where(left, x, turned), jnp.where(left, turned, x)

    def merge(k, ref, at, swap=None):
        a0 = acc_at(owner(k), core)

        def group(g, _):
            mine = pl.multiple_of(a0 + g * group_rows, SUB)
            theirs = pl.multiple_of(at + g * group_rows, SUB)

            def load(off):
                x = acc[pl.ds(pl.multiple_of(mine + off, SUB), SUB), :]
                y = ref[pl.ds(pl.multiple_of(theirs + off, SUB), SUB), :]
                if swap is not None:
                    x, y = jnp.where(swap, y, x), jnp.where(swap, x, y)
                return x, y

            x, y = load(stat)
            best_x, total_x = split(x)
            best_y, total_y = split(y)
            best = jnp.maximum(best_x, best_y)
            scale_x = jnp.exp(best_x - best)
            scale_y = jnp.exp(best_y - best)
            total = total_x * scale_x + total_y * scale_y
            acc[pl.ds(pl.multiple_of(mine + stat, SUB), SUB), :] = jnp.where(
                lane < LANES // 2, best, total
            )
            for j in range(tiles):
                x, y = load(j * SUB)
                acc[pl.ds(pl.multiple_of(mine + j * SUB, SUB), SUB), :] = x * scale_x + y * scale_y
            return 0

        lax.fori_loop(0, groups, group, 0)

    def acc_piece(k, half):
        return acc.at[pl.ds(acc_at(owner(k), half), piece), :]

    def slot_of(ref, k):
        return ref.at[pl.ds(k * piece, piece), :]

    core_copies = {}

    def share(k):
        core_copies[k] = remote(
            acc_piece(k, other), slot_of(rcore, k), rc_send.at[k], rc_recv.at[k], d_to(0)
        )

    def finish(k):
        core_copies[k].wait_recv()
        merge(k, rcore, k * piece)
        for b in range(low_bit(k) if k else nbits):
            j = k | 1 << b
            pltpu.make_async_remote_copy(
                src_ref=slot_of(rbits, j), dst_ref=slot_of(rbits, j), send_sem=rb_send.at[j],
                recv_sem=rb_recv.at[j], device_id=q_to(b), device_id_type=MESH,
            ).wait_recv()
            merge(k, rbits, j * piece)
        if k:
            remote(acc_piece(k, core), slot_of(rbits, k), rb_send.at[k], rb_recv.at[k], q_to(low_bit(k)))

    order = [0] + sorted(range(1, n), key=lambda k: (low_bit(k), k.bit_count(), k))
    own_copy.wait()
    late = None
    for k in order:
        while k and k in pending:
            relay(pending.pop(0))
        if k:
            arrived(k, other, agc_send, agc_recv, d_to(0))
        compute(k, other)
        share(k)
        compute(k, core)
        if late:
            finish(late)
        late = k
    finish(late)
    finish(0)

    for b in range(1, dbits):
        pltpu_copy = pltpu.make_async_remote_copy(
            src_ref=acc_piece(0, core), dst_ref=slot_of(rx, b), send_sem=rx_send.at[b],
            recv_sem=rx_recv.at[b], device_id=d_to(b), device_id_type=MESH,
        )
        pltpu_copy.start()
        pltpu_copy.wait()
        upper = jnp.full((SUB, LANES), lax.rem(dp // (1 << b), 2), jnp.int32)
        merge(0, rx, b * piece, swap=upper == 1)

    last = remote(acc_piece(0, core), fin, fin_send, fin_recv, d_to(0))

    def emit(ref, at, half):
        for g in range(groups):
            base = pl.multiple_of(at + g * group_rows, SUB)
            to = pl.multiple_of(half * half_rows + g * SUB, SUB)
            best, total = split(ref[pl.ds(pl.multiple_of(base + stat, SUB), SUB), :])
            log_ref[pl.ds(to, SUB), :] = best + jnp.log(total)
            inverse = 1.0 / total
            for j in range(tiles):
                out_ref[pl.ds(to, SUB), j * LANES : (j + 1) * LANES] = (
                    ref[pl.ds(pl.multiple_of(base + j * SUB, SUB), SUB), :] * inverse
                )

    emit(acc, acc_at(me, core), core)
    last.wait_recv()
    emit(fin, 0, other)
    for copy in started:
        copy.wait_send()


def body(corpus, queries, cand_ids, cand_counts):
    n, d = lax.axis_size("query"), lax.axis_size("dp")
    own, width = queries.shape
    slots = cand_ids.shape[2]
    rows = corpus.shape[0]
    tiles = width // LANES
    half_rows = own // 2
    inv_root = 1.0 / float(width) ** 0.5
    ids = cand_ids.reshape(-1)
    counts = cand_counts.reshape(-1)
    piece = half_rows // SUB * (tiles + 1) * SUB
    qpiece = half_rows * tiles
    dbits = d.bit_length() - 1
    f32 = jnp.float32
    dma = pltpu.SemaphoreType.DMA
    out, logs = pl.pallas_call(
        functools.partial(kernel, (n, d, half_rows, slots, tiles, rows, inv_root)),
        out_shape=(
            jax.ShapeDtypeStruct((own, width), f32),
            jax.ShapeDtypeStruct((own, LANES), f32),
        ),
        in_specs=[
            pl.BlockSpec(memory_space=pltpu.SMEM),
            pl.BlockSpec(memory_space=pltpu.SMEM),
            pl.BlockSpec(memory_space=pl.ANY),
            pl.BlockSpec(memory_space=pl.ANY),
        ],
        out_specs=(pl.BlockSpec(memory_space=pltpu.VMEM), pl.BlockSpec(memory_space=pltpu.VMEM)),
        scratch_shapes=[
            pltpu.VMEM((rows, tiles, LANES), f32),
            pltpu.VMEM((SLOTS, CHUNK, width), corpus.dtype),
            pltpu.VMEM((n * 2 * qpiece, LANES), f32),
            pltpu.VMEM((n * 2 * piece, LANES), f32),
            pltpu.VMEM((n * piece, LANES), f32),
            pltpu.VMEM((n * piece, LANES), f32),
            pltpu.VMEM((dbits * piece, LANES), f32),
            pltpu.VMEM((piece, LANES), f32),
            dma((SLOTS,)), dma, dma((n,)), dma((n,)), dma((n,)), dma((n,)),
            dma((n,)), dma((n,)), dma((n,)), dma((n,)), dma((dbits,)), dma((dbits,)), dma, dma,
        ],
        compiler_params=pltpu.CompilerParams(collective_id=0, has_side_effects=True),
        name="rescore",
    )(ids, counts, queries.reshape(own * tiles, LANES), corpus)
    return logs[:, 0], out


def solution(mesh):
    in_specs = (
        P(("dp", "query"), None),
        P("query", None),
        P(("dp", "query"), None, None),
        P(("dp", "query"), None),
    )
    out_specs = (P("query"), P("query", None))
    return jax.shard_map(body, mesh=mesh, in_specs=in_specs, out_specs=out_specs, check_vma=False)
```

time: 186 us -> 66.6 us (0.36)
  waiting for transfers between devices: 83.8 us -> 0 us
  Pallas kernels: 0 us -> 59.2 us
  matrix products: 28.4 us -> 0 us
  local copies, waits for them, and re-layouts: 32.5 us -> 6.35 us
  between operations: 14.8 us -> 0.65 us
  starting transfers between devices: 13 us -> 0 us
  blocking collectives: 9.18 us -> 0 us
  other arithmetic: 3.48 us -> 0 us
    pallas_call x0 -> x1, Pallas kernels: none -> 59.2 us  [body(): pl.pallas_call(functools.partial(kernel, (n, d, half_rows, slots, tiles,...]
    all_to_all x3 -> x0, waiting for transfers between devices: 49.7 us -> none  [the longest x1 45.1 us: body(): lax.all_to_all(part_weighted.reshape(n_owner, q_local, width), 'query', s...]
    all_gather x2 -> x0, waiting for transfers between devices: 33.4 us -> none  [the longest x1 25.1 us: body(): every_query = lax.all_gather(queries, 'query', axis=0, tiled=True)]
    dot_general x2 -> x0, matrix products: 28.4 us -> none  [the longest x1 19.1 us: body(): jnp.einsum('qcd,qd->qc', widened, every_query, precision=lax.Precision.HI...]
    gather x1 -> x0, local copies, waits for them, and re-layouts: 25.3 us -> none  [body(): picked = corpus[cand_ids[0]]]
    all_to_all x3 -> x0, starting transfers between devices: 12.9 us -> none  [the longest x1 5.37 us: body(): lax.all_to_all(part_weighted.reshape(n_owner, q_local, width), 'query', s...]
    unnamed x1 -> x0, blocking collectives: 9.18 us -> none
    reshape x0 -> x2, local copies, waits for them, and re-layouts: none -> 2.45 us  [the longest x1 1.7 us: body(): queries.reshape(own * tiles, LANES)]
  transfers between devices with their start and end apart: 5 -> 0, of which waited for: 4 -> 0; matrix products, arithmetic and copies ran while one was open for 21% -> 0% of each run, Pallas kernels for 0% -> 0%
where the time goes in v1:
time: 66.6 us; the launch traced here: 66.1 us
  Pallas kernels  59.2 us (89%)
  local copies, waits for them, and re-layouts  6.35 us (10%)
    pallas_call x1, Pallas kernels, body(): pl.pallas_call(functools.partial(kernel, (n, d, half_rows, slots, tiles,...  59.2 us
    unnamed x2, local copies, waits for them, and re-layouts  2.51 us
    reshape x1, local copies, waits for them, and re-layouts, body(): queries.reshape(own * tiles, LANES)  1.7 us
    slice x1, local copies, waits for them, and re-layouts, body(): return (logs[:, 0], out)  1.38 us

profile of v1, /device:TPU:1, one launch (start us, length us, event | category | flops | bytes accessed | tf_op | source)
XLA Modules:
  0.0 66.1 jit_solution(5208292013660548838)
XLA Ops:
  0.6 1.7 %reshape.15.q_hbm = f32[512,128]{1,0:T(8,128)} reshape(f32[64,1024]{1,0:T(8,128)} %param.5) | data formatting | bytes 524288 | tf_op jit(solution)/shard_map/reshape | solution.py:365
  2.3 0.8 %copy.6 = s32[1,512,8]{2,1,0:T(8,128)S(1)} copy(s32[1,512,8]{1,2,0:T(8,128)} %param.6) | data formatting | bytes 32768 | tf_op args[2]
  3.2 0.8 %reshape.13.ids = s32[4096]{0:T(1024)} reshape(s32[1,512,8]{2,1,0:T(8,128)S(1)} %copy.6) | data formatting | bytes 32768 | tf_op jit(solution)/shard_map/reshape | solution.py:331
  3.9 59.2 %rescore.1 = (f32[64,1024]{1,0:T(8,128)}, f32[64,128]{1,0:T(8,128)}) custom-call(s32[4096]{0:T(1024)} %reshape.13.ids, s32[512]{0:T(512)} %bitcast.1, f32[512,128]{1,0:T(8,128)} %reshape.15.q_hbm, bf16[4096,1024]{1,0:T(8,128)(2,1)} %corpus_hbm.1), custom_call_target="tpu_custom_call" | custom-call | tf_op jit(solution)/shard_map/rescore/pallas_call | solution.py:338
  63.1 1.4 %slice_reduce_fusion = f32[64]{0:T(128)} fusion(f32[64,128]{1,0:T(8,128)} %get-tuple-element.4), kind=kLoop, calls=%fused_computation | loop fusion | bytes 512 | tf_op jit(solution)/shard_map/slice | solution.py:366
  64.5 1.7 %copy.8 = f32[64,1024]{1,0:T(8,128)} copy(f32[64,1024]{1,0:T(8,128)} %get-tuple-element.9) | data formatting | bytes 524288

commit v2 on v1

--- a/solution.py
+++ b/solution.py
@@ -33,7 +33,8 @@
 
 def kernel(
     cfg, ids, counts, q_hbm, corpus_hbm, out_ref, log_ref,
-    c32, stage, allq, acc, rcore, rbits, rx, fin,
+    c32, stage, allq, acc, core_out, core_in, bits_out, bits_in,
+    core_out_stat, core_in_stat, bits_out_stat, bits_in_stat, rx, fin,
     stage_sem, own_sem, ag_send, ag_recv, agc_send, agc_recv,
     rc_send, rc_recv, rb_send, rb_recv, rx_send, rx_recv, fin_send, fin_recv,
 ):
@@ -49,6 +50,7 @@
     groups = half_rows // SUB
     piece = groups * group_rows
     qpiece = half_rows * tiles
+    own_lanes = log_ref.shape[1]
 
     def flip(x, bit):
         return x + (1 << bit) - 2 * (1 << bit) * lax.rem(x // (1 << bit), 2)
@@ -172,15 +174,15 @@
         first = s * (2 * half_rows) + half * half_rows
 
         def row(index):
-            return c32[ids[index]]
+            return c32[ids[index[1], index[0]]]
 
         def group(g, _):
             query = first + g * SUB
             weights, stats = [], jnp.zeros((SUB, LANES), jnp.float32)
             for qi in range(SUB):
-                at = (query + qi) * slots
+                at = query + qi
                 q = allq[pl.ds(pl.multiple_of(q0 + (g * SUB + qi) * tiles, SUB), tiles), :]
-                level = [row(at + c) * q for c in range(slots)]
+                level = [row((at, c)) * q for c in range(slots)]
                 for step in (1, 2, 4):
                     level = [
                         halves_combine(a, b, step, masks[step])
@@ -197,9 +199,9 @@
                 stats = jnp.where(sub == qi, jnp.where(lane < LANES // 2, best, total), stats)
             base = pl.multiple_of(a0 + g * group_rows, SUB)
             for qi in range(SUB):
-                at = (query + qi) * slots
+                at = query + qi
                 terms = [
-                    jnp.broadcast_to(weights[qi][c : c + 1, :], (SUB, LANES)) * row(at + c)
+                    jnp.broadcast_to(weights[qi][c : c + 1, :], (SUB, LANES)) * row((at, c))
                     for c in range(slots)
                 ]
                 while len(terms) > 1:
@@ -246,31 +248,111 @@
 
         lax.fori_loop(0, groups, group, 0)
 
+    fields = 3
+    field_lanes = LANES // (groups * fields)
+    prow = half_rows * tiles
+
+    def pack(k, half, data, stats):
+        a0 = acc_at(owner(k), half)
+
+        def group(g, packed):
+            base = pl.multiple_of(a0 + g * group_rows, SUB)
+            values = [acc[pl.ds(pl.multiple_of(base + j * SUB, SUB), SUB), :] for j in range(tiles)]
+            best, total = split(acc[pl.ds(pl.multiple_of(base + stat, SUB), SUB), :])
+            largest = functools.reduce(jnp.maximum, [jnp.abs(v) for v in values])
+            largest = jnp.maximum(jnp.max(largest, axis=1, keepdims=True), 1e-30)
+            largest = jnp.broadcast_to(largest, (SUB, LANES))
+            inverse = 32767.0 / largest
+            for j in range(0, tiles, 2):
+                x = jnp.concatenate([values[j] * inverse, values[j + 1] * inverse], axis=0)
+                at = pl.multiple_of(k * prow + g * (tiles * SUB) + j * SUB, 2 * SUB)
+                data[pl.ds(at, 2 * SUB), :] = jnp.round(x).astype(jnp.int32).astype(jnp.int16)
+            for f, x in enumerate((best, total, largest)):
+                packed = jnp.where(lane // field_lanes == g * fields + f, x, packed)
+            return packed
+
+        packed = lax.fori_loop(0, groups, group, jnp.zeros((SUB, LANES), jnp.float32))
+        stats[pl.ds(k * SUB, SUB), :] = packed
+
+    def merge_packed(k, data, stats, j_in):
+        a0 = acc_at(owner(k), core)
+        packed = stats[pl.ds(j_in * SUB, SUB), :]
+
+        def group(g, _):
+            base = pl.multiple_of(a0 + g * group_rows, SUB)
+
+            def field(f):
+                x = jnp.where(lane == (g * fields + f) * field_lanes, packed, 0.0)
+                return jnp.broadcast_to(jnp.sum(x, axis=1, keepdims=True), (SUB, LANES))
+
+            best_x, total_x = split(acc[pl.ds(pl.multiple_of(base + stat, SUB), SUB), :])
+            best_y, total_y, largest = field(0), field(1), field(2)
+            best = jnp.maximum(best_x, best_y)
+            scale_x = jnp.exp(best_x - best)
+            scale_y = jnp.exp(best_y - best)
+            total = total_x * scale_x + total_y * scale_y
+            acc[pl.ds(pl.multiple_of(base + stat, SUB), SUB), :] = jnp.where(
+                lane < LANES // 2, best, total
+            )
+            step_y = largest * (1.0 / 32767.0) * scale_y
+            for j in range(0, tiles, 2):
+                at = pl.multiple_of(j_in * prow + g * (tiles * SUB) + j * SUB, 2 * SUB)
+                y = data[pl.ds(at, 2 * SUB), :].astype(jnp.int32).astype(jnp.float32)
+                for i in range(2):
+                    to = pl.ds(pl.multiple_of(base + (j + i) * SUB, SUB), SUB)
+                    acc[to, :] = acc[to, :] * scale_x + y[i * SUB : (i + 1) * SUB] * step_y
+            return 0
+
+        lax.fori_loop(0, groups, group, 0)
+
+    def pair(k, source, source_stat, target, target_stat, send, recv, to):
+        rows_of, tile_of = pl.ds(k * prow, prow), pl.ds(k * SUB, SUB)
+        return (
+            pltpu.make_async_remote_copy(
+                src_ref=source.at[rows_of, :], dst_ref=target.at[rows_of, :],
+                send_sem=send.at[k], recv_sem=recv.at[k], device_id=to, device_id_type=MESH,
+            ),
+            pltpu.make_async_remote_copy(
+                src_ref=source_stat.at[tile_of, :], dst_ref=target_stat.at[tile_of, :],
+                send_sem=send.at[n + k], recv_sem=recv.at[n + k], device_id=to, device_id_type=MESH,
+            ),
+        )
+
+    def core_pair(k):
+        return pair(k, core_out, core_out_stat, core_in, core_in_stat, rc_send, rc_recv, d_to(0))
+
+    def bits_pair(k):
+        return pair(
+            k, bits_out, bits_out_stat, bits_in, bits_in_stat, rb_send, rb_recv, q_to(low_bit(k))
+        )
+
+    def launch(copies):
+        for copy in copies:
+            copy.start()
+            started.append(copy)
+
     def acc_piece(k, half):
         return acc.at[pl.ds(acc_at(owner(k), half), piece), :]
 
     def slot_of(ref, k):
         return ref.at[pl.ds(k * piece, piece), :]
 
-    core_copies = {}
-
     def share(k):
-        core_copies[k] = remote(
-            acc_piece(k, other), slot_of(rcore, k), rc_send.at[k], rc_recv.at[k], d_to(0)
-        )
+        pack(k, other, core_out, core_out_stat)
+        launch(core_pair(k))
 
     def finish(k):
-        core_copies[k].wait_recv()
-        merge(k, rcore, k * piece)
+        for copy in core_pair(k):
+            copy.wait_recv()
+        merge_packed(k, core_in, core_in_stat, k)
         for b in range(low_bit(k) if k else nbits):
             j = k | 1 << b
-            pltpu.make_async_remote_copy(
-                src_ref=slot_of(rbits, j), dst_ref=slot_of(rbits, j), send_sem=rb_send.at[j],
-                recv_sem=rb_recv.at[j], device_id=q_to(b), device_id_type=MESH,
-            ).wait_recv()
-            merge(k, rbits, j * piece)
+            for copy in bits_pair(j):
+                copy.wait_recv()
+            merge_packed(k, bits_in, bits_in_stat, j)
         if k:
-            remote(acc_piece(k, core), slot_of(rbits, k), rb_send.at[k], rb_recv.at[k], q_to(low_bit(k)))
+            pack(k, core, bits_out, bits_out_stat)
+            launch(bits_pair(k))
 
     order = [0] + sorted(range(1, n), key=lambda k: (low_bit(k), k.bit_count(), k))
     own_copy.wait()
@@ -301,12 +383,17 @@
 
     last = remote(acc_piece(0, core), fin, fin_send, fin_recv, d_to(0))
 
+    logs = []
+    wide = lax.broadcasted_iota(jnp.int32, (SUB, own_lanes), 1)
+    deep = lax.broadcasted_iota(jnp.int32, (SUB, own_lanes), 0)
+
     def emit(ref, at, half):
         for g in range(groups):
             base = pl.multiple_of(at + g * group_rows, SUB)
             to = pl.multiple_of(half * half_rows + g * SUB, SUB)
             best, total = split(ref[pl.ds(pl.multiple_of(base + stat, SUB), SUB), :])
-            log_ref[pl.ds(to, SUB), :] = best + jnp.log(total)
+            value = (best + jnp.log(total))[:, :1]
+            logs.append(jnp.where(wide == to + deep, value, 0.0))
             inverse = 1.0 / total
             for j in range(tiles):
                 out_ref[pl.ds(to, SUB), j * LANES : (j + 1) * LANES] = (
@@ -316,6 +403,7 @@
     emit(acc, acc_at(me, core), core)
     last.wait_recv()
     emit(fin, 0, other)
+    log_ref[...] = jnp.sum(functools.reduce(jnp.add, logs), axis=0, keepdims=True)
     for copy in started:
         copy.wait_send()
 
@@ -328,7 +416,7 @@
     tiles = width // LANES
     half_rows = own // 2
     inv_root = 1.0 / float(width) ** 0.5
-    ids = cand_ids.reshape(-1)
+    ids = cand_ids[0].T
     counts = cand_counts.reshape(-1)
     piece = half_rows // SUB * (tiles + 1) * SUB
     qpiece = half_rows * tiles
@@ -339,7 +427,7 @@
         functools.partial(kernel, (n, d, half_rows, slots, tiles, rows, inv_root)),
         out_shape=(
             jax.ShapeDtypeStruct((own, width), f32),
-            jax.ShapeDtypeStruct((own, LANES), f32),
+            jax.ShapeDtypeStruct((1, own), f32),
         ),
         in_specs=[
             pl.BlockSpec(memory_space=pltpu.SMEM),
@@ -353,17 +441,17 @@
             pltpu.VMEM((SLOTS, CHUNK, width), corpus.dtype),
             pltpu.VMEM((n * 2 * qpiece, LANES), f32),
             pltpu.VMEM((n * 2 * piece, LANES), f32),
-            pltpu.VMEM((n * piece, LANES), f32),
-            pltpu.VMEM((n * piece, LANES), f32),
+            *[pltpu.VMEM((n * qpiece, LANES), jnp.int16)] * 4,
+            *[pltpu.VMEM((n * SUB, LANES), f32)] * 4,
             pltpu.VMEM((dbits * piece, LANES), f32),
             pltpu.VMEM((piece, LANES), f32),
             dma((SLOTS,)), dma, dma((n,)), dma((n,)), dma((n,)), dma((n,)),
-            dma((n,)), dma((n,)), dma((n,)), dma((n,)), dma((dbits,)), dma((dbits,)), dma, dma,
+            *[dma((2 * n,))] * 4, dma((dbits,)), dma((dbits,)), dma, dma,
         ],
         compiler_params=pltpu.CompilerParams(collective_id=0, has_side_effects=True),
         name="rescore",
     )(ids, counts, queries.reshape(own * tiles, LANES), corpus)
-    return logs[:, 0], out
+    return logs[0], out
 
 
 def solution(mesh):

time: 66.6 us -> 64.3 us (0.965)
  local copies, waits for them, and re-layouts: 6.35 us -> 4.5 us
    slice x1 -> x0, local copies, waits for them, and re-layouts: 1.38 us -> none  [body(): return (logs[:, 0], out)]
    reshape x1 -> x0, local copies, waits for them, and re-layouts: 0.76 us -> none  [body(): ids = cand_ids.reshape(-1)]
where the time goes in v2:
time: 64.3 us; the launch traced here: 63.9 us
  Pallas kernels  58.8 us (91%)
  local copies, waits for them, and re-layouts  4.5 us (7%)
    pallas_call x1, Pallas kernels, body(): pl.pallas_call(functools.partial(kernel, (n, d, half_rows, slots, tiles,...  58.8 us
    unnamed x2, local copies, waits for them, and re-layouts  2.8 us
    reshape x1, local copies, waits for them, and re-layouts, body(): queries.reshape(own * tiles, LANES)  1.7 us

profile of v2, /device:TPU:1, one launch (start us, length us, event | category | flops | bytes accessed | tf_op | source)
XLA Modules:
  0.0 63.9 jit_solution(12863500438016712761)
XLA Ops:
  0.6 1.7 %reshape.11.q_hbm = f32[512,128]{1,0:T(8,128)} reshape(f32[64,1024]{1,0:T(8,128)} %param.5) | data formatting | bytes 524288 | tf_op jit(solution)/shard_map/reshape | solution.py:453
  2.3 58.8 %rescore.1 = (f32[64,1024]{1,0:T(8,128)}, f32[1,64]{1,0:T(1,128)}) custom-call(s32[8,512]{1,0:T(8,128)} %bitcast.5, s32[512]{0:T(512)} %bitcast.6, f32[512,128]{1,0:T(8,128)} %reshape.11.q_hbm, bf16[4096,1024]{1,0:T(8,128)(2,1)} %corpus_hbm.1), custom_call_target="tpu_custom_call" | custom-call | tf_op jit(solution)/shard_map/rescore/pallas_call | solution.py:426
  61.1 1.1 %copy.8 = f32[64]{0:T(128)} copy(f32[64]{0:T(128)} %bitcast.7) | data formatting | bytes 512
  62.3 1.7 %copy.9 = f32[64,1024]{1,0:T(8,128)} copy(f32[64,1024]{1,0:T(8,128)} %get-tuple-element.9) | data formatting | bytes 524288

commit v3 on v2

--- a/solution.py
+++ b/solution.py
@@ -210,7 +210,7 @@
             acc[pl.ds(pl.multiple_of(base + stat, SUB), SUB), :] = stats
             return 0
 
-        lax.fori_loop(0, groups, group, 0)
+        lax.fori_loop(0, groups, group, 0, unroll=2)
 
     def split(x):
         turned = pltpu.roll(x, LANES // 2, 1)
@@ -246,7 +246,7 @@
                 acc[pl.ds(pl.multiple_of(mine + j * SUB, SUB), SUB), :] = x * scale_x + y * scale_y
             return 0
 
-        lax.fori_loop(0, groups, group, 0)
+        lax.fori_loop(0, groups, group, 0, unroll=True)
 
     fields = 3
     field_lanes = LANES // (groups * fields)
@@ -271,7 +271,7 @@
                 packed = jnp.where(lane // field_lanes == g * fields + f, x, packed)
             return packed
 
-        packed = lax.fori_loop(0, groups, group, jnp.zeros((SUB, LANES), jnp.float32))
+        packed = lax.fori_loop(0, groups, group, jnp.zeros((SUB, LANES), jnp.float32), unroll=True)
         stats[pl.ds(k * SUB, SUB), :] = packed
 
     def merge_packed(k, data, stats, j_in):
@@ -303,7 +303,7 @@
                     acc[to, :] = acc[to, :] * scale_x + y[i * SUB : (i + 1) * SUB] * step_y
             return 0
 
-        lax.fori_loop(0, groups, group, 0)
+        lax.fori_loop(0, groups, group, 0, unroll=True)
 
     def pair(k, source, source_stat, target, target_stat, send, recv, to):
         rows_of, tile_of = pl.ds(k * prow, prow), pl.ds(k * SUB, SUB)
@@ -364,9 +364,9 @@
             arrived(k, other, agc_send, agc_recv, d_to(0))
         compute(k, other)
         share(k)
-        compute(k, core)
         if late:
             finish(late)
+        compute(k, core)
         late = k
     finish(late)
     finish(0)

time: 64.3 us -> 56.2 us (0.87)
  Pallas kernels: 58.8 us -> 50.7 us
    pallas_call x1, Pallas kernels: 58.8 us -> 50.7 us  [body(): pl.pallas_call(functools.partial(kernel, (n, d, half_rows, slots, tiles,...]
where the time goes in v3:
time: 56.2 us; the launch traced here: 55.9 us
  Pallas kernels  50.7 us (90%)
  local copies, waits for them, and re-layouts  4.5 us (8%)
  between operations  0.64 us (1%)
    pallas_call x1, Pallas kernels, body(): pl.pallas_call(functools.partial(kernel, (n, d, half_rows, slots, tiles,...  50.7 us
    unnamed x2, local copies, waits for them, and re-layouts  2.8 us
    reshape x1, local copies, waits for them, and re-layouts, body(): queries.reshape(own * tiles, LANES)  1.7 us

profile of v3, /device:TPU:1, one launch (start us, length us, event | category | flops | bytes accessed | tf_op | source)
XLA Modules:
  0.0 55.9 jit_solution(2012720213337973182)
XLA Ops:
  0.6 1.7 %reshape.11.q_hbm = f32[512,128]{1,0:T(8,128)} reshape(f32[64,1024]{1,0:T(8,128)} %param.5) | data formatting | bytes 524288 | tf_op jit(solution)/shard_map/reshape | solution.py:453
  2.3 50.7 %rescore.1 = (f32[64,1024]{1,0:T(8,128)}, f32[1,64]{1,0:T(1,128)}) custom-call(s32[8,512]{1,0:T(8,128)} %bitcast.5, s32[512]{0:T(512)} %bitcast.6, f32[512,128]{1,0:T(8,128)} %reshape.11.q_hbm, bf16[4096,1024]{1,0:T(8,128)(2,1)} %corpus_hbm.1), custom_call_target="tpu_custom_call" | custom-call | tf_op jit(solution)/shard_map/rescore/pallas_call | solution.py:426
  53.1 1.1 %copy.8 = f32[64]{0:T(128)} copy(f32[64]{0:T(128)} %bitcast.7) | data formatting | bytes 512
  54.2 1.7 %copy.9 = f32[64,1024]{1,0:T(8,128)} copy(f32[64,1024]{1,0:T(8,128)} %get-tuple-element.9) | data formatting | bytes 524288
